TPU v7x, 32 devices: a whole 2x2x4 slice. The times are simulated.
32 devices in a mesh: tm: 4 (over z), rows: 8 (over y, x, core).
Axes of the slice: x: 2, y: 2, z: 4, core: 2. Of those that a mesh axis runs over, the one named last changes fastest.
Arguments:
- snapshots: float32 [196608, 256], P('rows', 'tm'), may hold values from -100 to 100
- last_snapshot: float32 [196608], P('rows'), may hold values from -100 to 100
Outputs:
- basis_rows: float32 [8, 4, 6144, 256], P('rows', 'tm')
- factor: float32 [256, 256], replicated
- projected: float32 [256, 256], replicated
- operator: float32 [256, 256], replicated
All inputs are finite; a program needn't handle non-finite values.
Results may differ from a plain program's by a relative error of at most 0.0003.
Values sent between devices are 32-bit elements; how exact they have to be, the bound alone decides.
No kernel may reach another device: no remote copies, remote signals or barrier semaphores. Data moves between devices by JAX's collectives and lax.ppermute only.
A program may use at most 128 MiB of HBM per device.

v0:
```python
import jax
import jax.numpy as jnp
from jax import lax
from jax.sharding import PartitionSpec as P


def sum_moments(first_part, second_part):
    first_total, second_total = lax.psum((first_part, second_part), ("tm", "rows"))
    return (first_total, second_total)


def shards(snapshots, last_snapshot):
    highest = lax.Precision.HIGHEST
    local_rows = lax.all_to_all(snapshots, "tm", split_axis=0, concat_axis=1, tiled=True)
    row_count = local_rows.shape[0]
    col_count = local_rows.shape[1]
    last_column = lax.dynamic_slice_in_dim(
        last_snapshot, lax.axis_index("tm") * row_count, row_count, 0
    )
    gram_part = jnp.dot(
        local_rows.T, local_rows, precision=highest, preferred_element_type=jnp.float32
    )
    tail_part = jnp.dot(
        last_column, local_rows, precision=highest, preferred_element_type=jnp.float32
    )
    gram_total, tail_total = sum_moments(gram_part, tail_part)
    samples = row_count * lax.axis_size("tm") * lax.axis_size("rows")
    gram_matrix = gram_total / samples
    tail_column = tail_total / samples
    cross_matrix = jnp.concatenate([gram_matrix[:, 1:], tail_column[:, None]], axis=1)
    lower_factor = jnp.linalg.cholesky(gram_matrix)
    identity = jnp.eye(col_count, dtype=jnp.float32)
    inverse = jax.scipy.linalg.solve_triangular(lower_factor, identity, lower=True)
    factor = lower_factor.T
    basis_rows = jnp.dot(
        local_rows, inverse.T, precision=highest, preferred_element_type=jnp.float32
    )
    projected = jnp.dot(
        inverse, cross_matrix, precision=highest, preferred_element_type=jnp.float32
    )
    operator = jnp.dot(projected, inverse.T, precision=highest, preferred_element_type=jnp.float32)
    return (basis_rows.reshape(1, 1, row_count, col_count), factor, projected, operator)


def solution(mesh):
    in_specs = (P("rows", "tm"), P("rows"))
    out_specs = (P("rows", "tm", None, None), P(), P(), P())
    return jax.shard_map(shards, mesh=mesh, in_specs=in_specs, out_specs=out_specs, check_vma=False)
```

profile of v0, /device:TPU:0, one launch (start us, length us, event | category | flops | bytes accessed | tf_op | source)
XLA Modules:
  0.0 436.9 jit_solution(7543601814728142755)
XLA Ops:
  7.2 6.2 %copy.27 = f32[8,4,8,6144]{3,2,0,1:T(8,128)} copy(f32[8,4,8,6144]{3,2,1,0:T(8,128)} %bitcast.54) | data formatting | bytes 12582912 | tf_op jit(solution)/shard_map/all_to_all | solution.py:14
  13.4 6.3 %all-to-all-start = ((f32[4,6144,64]{1,2,0:T(8,128)}), f32[4,6144,64]{1,2,0:T(8,128)}, u32[]{:S(2)}, u32[]{:S(2)}) async-start(f32[4,6144,64]{1,2,0:T(8,128)} %bitcast.53), calls=%async_computation | async-start | bytes 12582912 | tf_op jit(solution)/shard_map/all_to_all | solution.py:14
  19.8 138.7 %all-to-all-done = f32[4,6144,64]{1,2,0:T(8,128)} async-done(((f32[4,6144,64]{1,2,0:T(8,128)}), f32[4,6144,64]{1,2,0:T(8,128)}, u32[]{:S(2)}, u32[]{:S(2)}) %all-to-all-start) | async-done | bytes 6291488 | tf_op jit(solution)/shard_map/all_to_all | solution.py:14
  158.4 17.7 %fusion.19 = f32[256,256]{0,1:T(8,128)} fusion(f32[6144,256]{0,1:T(8,128)} %bitcast.1), kind=kOutput, calls=%fused_computation.44 | convolution fusion | flops 4831838208 | bytes 6553600 | tf_op jit(solution)/shard_map/dot_general | solution.py:20
  176.2 7.0 %fusion.20 = f32[1,256]{1,0:T(1,128)S(1)} fusion(f32[6144,1]{0,1:T(1,128)S(1)} %bitcast.55, f32[6144,256]{0,1:T(8,128)} %bitcast.1), kind=kOutput, calls=%fused_computation.45 | convolution fusion | flops 18874368 | bytes 6317056 | tf_op jit(solution)/shard_map/dot_general | solution.py:23
  183.1 38.1 %psum.15 = f32[256]{0:T(256)S(1)} all-reduce(f32[256]{0:T(256)S(1)} %bitcast.57), channel_id=1, replica_groups=mesh['tm'=4,'rows'=8] {'tm','rows'}, use_global_device_ids=true, to_apply=%region_5.6 | all-reduce | flops 256 | bytes 2048 | tf_op jit(solution)/shard_map/psum | solution.py:8
  221.2 0.0 all-reduce.3.cloned.1.call-update
  221.2 125.6 %all-reduce.3.cloned.1.call-done = f32[256,256]{0,1:T(8,128)} async-done(((f32[256,256]{0,1:T(8,128)}), f32[256,256]{0,1:T(8,128)}) %all-reduce.3.cloned.1.call-update) | async-done | bytes 262160 | tf_op jit(solution)/shard_map/psum | solution.py:8
  346.8 1.0 broadcast_multiply_fusion
  347.8 0.1 copy.21
  347.9 1.0 fusion.4
  348.9 11.7 %cholesky.50 = f32[128,128]{1,0:T(8,128)S(1)} custom-call(f32[128,128]{1,0:T(8,128)S(1)} %cholesky.118), custom_call_target="Cholesky" | custom-call | tf_op jit(solution)/shard_map/jit(cholesky)/cholesky | solution.py:31
  360.7 9.8 %custom-call.15 = f32[1,128,128]{1,2,0:T(8,128)S(1)} custom-call(f32[1,128,128]{2,1,0:T(8,128)S(1)} %get-tuple-element.43), custom_call_target="InvertDiagBlocksLowerTriangular" | custom-call | tf_op jit(solution)/shard_map/jit(cholesky)/cholesky | solution.py:31
  370.5 0.2 constant_dynamic-update-slice_fusion.1
  370.8 0.3 convolution_subtract_fusion.1
  371.0 11.7 %cholesky.105 = f32[128,128]{1,0:T(8,128)S(1)} custom-call(f32[128,128]{1,0:T(8,128)S(1)} %convolution_subtract_fusion.1), custom_call_target="Cholesky" | custom-call | tf_op jit(solution)/shard_map/jit(cholesky)/cholesky | solution.py:31
  382.8 0.6 compare_reduce_fusion
  384.8 0.8 copy.23
  385.6 0.1 triangular_solve.63
  385.7 4.0 while.1
  385.7 0.6 fusion.32
  386.3 1.4 bitcast_dynamic-update-slice_fusion.2
  387.7 0.6 fusion.32
  388.3 1.4 bitcast_dynamic-update-slice_fusion.2
  389.7 19.9 %custom-call.16 = f32[2,128,128]{1,2,0:T(8,128)S(1)} custom-call(f32[2,128,128]{2,1,0:T(8,128)S(1)} %get-tuple-element.11), custom_call_target="InvertDiagBlocksLowerTriangular" | custom-call | tf_op jit(solution)/shard_map/jit(_solve_triangular)/triangular_solve | solution.py:33
  409.6 0.3 fusion.8
  409.8 0.3 convolution_subtract_fusion
  410.1 0.3 fusion.11
  410.4 11.5 %convolution_bitcast_fusion = f32[1,1,6144,256]{2,3,1,0:T(8,128)} fusion(f32[6144,256]{0,1:T(8,128)} %bitcast.1, f32[128,256]{1,0:T(8,128)S(1)} %fusion.11, f32[128,256]{1,0:T(8,128)S(1)} %fusion.8), kind=kOutput, calls=%fused_computation.2 | convolution fusion | flops 4831903744 | bytes 12845056 | tf_op jit(solution)/shard_map/dot_general | solution.py:35
  421.9 0.4 fusion
  422.4 1.1 fusion.7
  423.5 6.6 %copy.22 = f32[1,1,6144,256]{3,2,1,0:T(8,128)} copy(f32[1,1,6144,256]{2,3,1,0:T(8,128)} %convolution_bitcast_fusion) | data formatting | bytes 12582912
  (18 shorter events, 0.2 us)
Async XLA Ops:
  7.2 12.5 %copy-start = (f32[24576]{0:T(1024)S(1)}, f32[24576]{0:T(1024)}, u32[]{:S(2)}) copy-start(f32[24576]{0:T(1024)} %param.3) | copy-start | bytes 294916
  13.4 145.1 %all-to-all-start = ((f32[4,6144,64]{1,2,0:T(8,128)}), f32[4,6144,64]{1,2,0:T(8,128)}, u32[]{:S(2)}, u32[]{:S(2)}) async-start(f32[4,6144,64]{1,2,0:T(8,128)} %bitcast.53), calls=%async_computation | async-start | bytes 12582912 | tf_op jit(solution)/shard_map/all_to_all | solution.py:14
  19.7 327.1 %all-reduce.3.cloned.1.call-start = ((), (), s32[]{:S(2)}) async-start(), calls=%async_computation.1 | async-start | bytes 524288 | tf_op jit(solution)/shard_map/psum | solution.py:8
  422.3 7.7 %copy-start.1 = (f32[256,256]{1,0:T(8,128)}, f32[256,256]{1,0:T(8,128)S(1)}, u32[]{:S(2)}) copy-start(f32[256,256]{1,0:T(8,128)S(1)} %fusion) | copy-start | bytes 786436
Sparse Core Ops, SparseCore 0:
  221.4 125.3 all-reduce.2
where the time goes:
time: 437 us
  waiting for transfers between devices  264 us (60%)
  other arithmetic  55.9 us (13%)
  matrix products  39 us (9%)
  blocking collectives  38.1 us (9%)
  local copies, waits for them, and re-layouts  17.8 us (4%)
  between operations  15.5 us (4%)
  starting transfers between devices  6.32 us (1%)
    all_to_all x1, waiting for transfers between devices, shards(): lax.all_to_all(snapshots, 'tm', split_axis=0, concat_axis=1, tiled=True)  139 us
    psum x1, waiting for transfers between devices, sum_moments(): lax.psum((first_part, second_part), ('tm', 'rows'))  126 us
    psum x1, blocking collectives, sum_moments(): lax.psum((first_part, second_part), ('tm', 'rows'))  38.1 us
    another operation x6, other arithmetic, shards(): lower_factor = jnp.linalg.cholesky(gram_matrix)  34 us
    another operation x2, other arithmetic, shards(): jax.scipy.linalg.solve_triangular(lower_factor, identity, lower=True)  19.9 us
    dot_general x1, matrix products, shards(): jnp.dot(local_rows.T, local_rows, precision=highest, preferred_element_ty...  17.7 us
    dot_general x1, matrix products, shards(): jnp.dot(local_rows, inverse.T, precision=highest, preferred_element_type=...  11.5 us
  transfers between devices with their start and end apart: 2, of which 2 were waited for; matrix products, arithmetic and copies ran while one was open for 0% of the time, Pallas kernels for 0%

commit v1 on v0

--- a/solution.py
+++ b/solution.py
@@ -5,7 +5,13 @@
 
 
 def sum_moments(first_part, second_part):
-    first_total, second_total = lax.psum((first_part, second_part), ("tm", "rows"))
+
+    def resolve_limits(mat):
+        for jj in ("rows", "tm"):
+            mat = lax.psum(mat, axis_name=jj)
+        return mat
+
+    first_total, second_total = resolve_limits((first_part, second_part))
     return (first_total, second_total)
 
 

time: 437 us -> 344 us (0.79)
  waiting for transfers between devices: 264 us -> 59.1 us
  blocking collectives: 38.1 us -> 168 us
  matrix products: 39 us -> 27.3 us
  starting transfers between devices: 6.32 us -> 0.08 us
    all_to_all x0 -> x1, blocking collectives: none -> 144 us  [shards(): lax.all_to_all(snapshots, 'tm', split_axis=0, concat_axis=1, tiled=True)]
    all_to_all x1 -> x0, waiting for transfers between devices: 139 us -> none  [shards(): lax.all_to_all(snapshots, 'tm', split_axis=0, concat_axis=1, tiled=True)]
    psum x1 -> x2, waiting for transfers between devices: 126 us -> 59.1 us  [resolve_limits(): mat = lax.psum(mat, axis_name=jj)]
    psum x1 -> x2, blocking collectives: 38.1 us -> 24.1 us  [resolve_limits(): mat = lax.psum(mat, axis_name=jj)]
    dot_general x1, matrix products: 17.7 us -> 5.89 us  [shards(): jnp.dot(local_rows.T, local_rows, precision=highest, preferred_element_ty...]
    all_to_all x1 -> x0, starting transfers between devices: 6.32 us -> none  [shards(): lax.all_to_all(snapshots, 'tm', split_axis=0, concat_axis=1, tiled=True)]
    unnamed x6 -> x8, local copies, waits for them, and re-layouts: 7.41 us -> 10.1 us
  transfers between devices with their start and end apart: 2 -> 2, of which waited for: 2 -> 2; matrix products, arithmetic and copies ran while one was open for 0% -> 2% of each run, Pallas kernels for 0% -> 0%
where the time goes in v1:
time: 344 us
  blocking collectives  168 us (49%)
  waiting for transfers between devices  59.1 us (17%)
  other arithmetic  55.9 us (16%)
  matrix products  27.3 us (8%)
  local copies, waits for them, and re-layouts  17.6 us (5%)
  between operations  15.5 us (5%)
    all_to_all x1, blocking collectives, shards(): lax.all_to_all(snapshots, 'tm', split_axis=0, concat_axis=1, tiled=True)  144 us
    psum x2, waiting for transfers between devices, resolve_limits(): mat = lax.psum(mat, axis_name=jj)  59.1 us
    another operation x6, other arithmetic, shards(): lower_factor = jnp.linalg.cholesky(gram_matrix)  34 us
    psum x2, blocking collectives, resolve_limits(): mat = lax.psum(mat, axis_name=jj)  24.1 us
    another operation x2, other arithmetic, shards(): jax.scipy.linalg.solve_triangular(lower_factor, identity, lower=True)  19.9 us
    dot_general x1, matrix products, shards(): jnp.dot(local_rows, inverse.T, precision=highest, preferred_element_type=...  11.6 us
    unnamed x8, local copies, waits for them, and re-layouts  10.1 us
    dot_general x1, matrix products, shards(): jnp.dot(last_column, local_rows, precision=highest, preferred_element_typ...  6.98 us
  transfers between devices with their start and end apart: 2, of which 2 were waited for; matrix products, arithmetic and copies ran while one was open for 2% of the time, Pallas kernels for 0%

profile of v1, /device:TPU:0, one launch (start us, length us, event | category | flops | bytes accessed | tf_op | source)
XLA Modules:
  0.0 343.9 jit_solution(687304196923190433)
XLA Ops:
  7.2 3.2 copy.27
  10.5 144.2 %all_to_all.19 = f32[4,6144,64]{1,2,0:T(8,128)S(1)} all-to-all(f32[4,6144,64]{1,2,0:T(8,128)S(1)} %bitcast.56), channel_id=1, replica_groups=mesh['tm'=4,'rows'=8] {'tm'}, dimensions={0} | all-to-all | bytes 12582912 | tf_op jit(solution)/shard_map/all_to_all | solution.py:20
  154.7 2.7 copy-done.1
  157.4 5.9 %fusion.19 = f32[256,256]{0,1:T(8,128)} fusion(f32[6144,256]{0,1:T(8,128)S(1)} %bitcast.53), kind=kOutput, calls=%fused_computation.44 | convolution fusion | flops 4831838208 | bytes 6553600 | tf_op jit(solution)/shard_map/dot_general | solution.py:26
  163.4 53.0 %all-reduce.4.cloned.1.call-done = f32[256,256]{0,1:T(8,128)} async-done(((f32[256,256]{0,1:T(8,128)}), f32[256,256]{0,1:T(8,128)}) %all-reduce.4.cloned.1.call-update) | async-done | bytes 262160 | tf_op jit(solution)/shard_map/psum | solution.py:11
  216.5 7.0 %fusion.20 = f32[1,256]{1,0:T(1,128)S(1)} fusion(f32[6144,1]{0,1:T(1,128)S(1)} %bitcast.58, f32[6144,256]{0,1:T(8,128)} %bitcast.54), kind=kOutput, calls=%fused_computation.45 | convolution fusion | flops 18874368 | bytes 6317056 | tf_op jit(solution)/shard_map/dot_general | solution.py:29
  223.5 11.8 %psum.30 = f32[256]{0:T(256)S(1)} all-reduce(f32[256]{0:T(256)S(1)} %bitcast.60), channel_id=1, replica_groups=mesh['tm'=4,'rows'=8] {'rows'}, use_global_device_ids=true, to_apply=%region_6.7 | all-reduce | flops 256 | bytes 2048 | tf_op jit(solution)/shard_map/psum | solution.py:11
  235.3 12.3 %psum.31 = f32[256]{0:T(256)S(1)} all-reduce(f32[256]{0:T(256)S(1)} %psum.30), channel_id=1, replica_groups=mesh['tm'=4,'rows'=8] {'tm'}, use_global_device_ids=true, to_apply=%region_7.8 | all-reduce | flops 256 | bytes 2048 | tf_op jit(solution)/shard_map/psum | solution.py:11
  247.5 6.1 %all-reduce.6.cloned.1.call-done = f32[256,256]{0,1:T(8,128)} async-done(((f32[256,256]{0,1:T(8,128)}), f32[256,256]{0,1:T(8,128)}) %all-reduce.6.cloned.1.call-update) | async-done | bytes 262160 | tf_op jit(solution)/shard_map/psum | solution.py:11
  253.6 1.0 broadcast_multiply_fusion
  254.6 0.1 copy.21
  254.7 1.0 fusion.4
  255.8 11.7 %cholesky.50 = f32[128,128]{1,0:T(8,128)S(1)} custom-call(f32[128,128]{1,0:T(8,128)S(1)} %cholesky.118), custom_call_target="Cholesky" | custom-call | tf_op jit(solution)/shard_map/jit(cholesky)/cholesky | solution.py:37
  267.5 9.8 %custom-call.15 = f32[1,128,128]{1,2,0:T(8,128)S(1)} custom-call(f32[1,128,128]{2,1,0:T(8,128)S(1)} %get-tuple-element.43), custom_call_target="InvertDiagBlocksLowerTriangular" | custom-call | tf_op jit(solution)/shard_map/jit(cholesky)/cholesky | solution.py:37
  277.3 0.2 constant_dynamic-update-slice_fusion.1
  277.6 0.3 convolution_subtract_fusion.1
  277.8 11.7 %cholesky.105 = f32[128,128]{1,0:T(8,128)S(1)} custom-call(f32[128,128]{1,0:T(8,128)S(1)} %convolution_subtract_fusion.1), custom_call_target="Cholesky" | custom-call | tf_op jit(solution)/shard_map/jit(cholesky)/cholesky | solution.py:37
  289.6 0.6 compare_reduce_fusion
  291.6 0.8 copy.23
  292.5 4.1 %while.1 = (s32[]{:T(128)}, f32[256,256]{1,0:T(8,128)S(1)}, s32[2,2]{1,0:T(2,128)S(1)}, f32[2,128,128]{2,1,0:T(8,128)S(1)}, s32[]{:T(128)}) while((s32[]{:T(128)}, f32[256,256]{1,0:T(8,128)S(1)}, s32[2,2]{1,0:T(2,128)S(1)}, f32[2,128,128]{2,1,0:T(8,128)S(1)}, s32[]{:T(128)}) %tuple.32), condition=%wide.while_cond, body=%wide.while_body.sunk | while | flops 2 | bytes 131189 | solution.py:39
  292.5 0.6 fusion.32
  293.1 1.4 bitcast_dynamic-update-slice_fusion.2
  294.5 0.6 fusion.32
  295.1 1.4 bitcast_dynamic-update-slice_fusion.2
  296.6 19.9 %custom-call.16 = f32[2,128,128]{1,2,0:T(8,128)S(1)} custom-call(f32[2,128,128]{2,1,0:T(8,128)S(1)} %get-tuple-element.11), custom_call_target="InvertDiagBlocksLowerTriangular" | custom-call | tf_op jit(solution)/shard_map/jit(_solve_triangular)/triangular_solve | solution.py:39
  316.5 0.3 fusion.8
  316.8 0.3 convolution_subtract_fusion
  317.0 0.3 fusion.11
  317.3 11.6 %convolution_bitcast_fusion = f32[1,1,6144,256]{2,3,1,0:T(8,128)} fusion(f32[6144,256]{0,1:T(8,128)} %bitcast.55, f32[128,256]{1,0:T(8,128)S(1)} %fusion.11, f32[128,256]{1,0:T(8,128)S(1)} %fusion.8), kind=kOutput, calls=%fused_computation.2 | convolution fusion | flops 4831903744 | bytes 12845056 | tf_op jit(solution)/shard_map/dot_general | solution.py:41
  328.9 0.4 fusion
  329.4 1.1 fusion.7
  330.5 6.6 %copy.22 = f32[1,1,6144,256]{3,2,1,0:T(8,128)} copy(f32[1,1,6144,256]{2,3,1,0:T(8,128)} %convolution_bitcast_fusion) | data formatting | bytes 12582912
  (23 shorter events, 0.4 us)
Async XLA Ops:
  7.2 156.2 %copy-start = (f32[24576]{0:T(1024)S(1)}, f32[24576]{0:T(1024)}, u32[]{:S(2)}) copy-start(f32[24576]{0:T(1024)} %param.3) | copy-start | bytes 294916
  7.2 209.3 %all-reduce.4.cloned.1.call-start = ((), (), s32[]{:S(2)}) async-start(), calls=%async_computation.1 | async-start | bytes 524288 | tf_op jit(solution)/shard_map/psum | solution.py:11
  154.7 2.7 copy-start.1
  163.3 90.3 %all-reduce.6.cloned.1.call-start = ((), (), s32[]{:S(2)}) async-start(), calls=%async_computation.2 | async-start | bytes 524288 | tf_op jit(solution)/shard_map/psum | solution.py:11
  329.3 7.7 %copy-start.2 = (f32[256,256]{1,0:T(8,128)}, f32[256,256]{1,0:T(8,128)S(1)}, u32[]{:S(2)}) copy-start(f32[256,256]{1,0:T(8,128)S(1)} %fusion) | copy-start | bytes 786436
Sparse Core Ops, SparseCore 0:
  163.4 53.0 all-reduce.3
  218.9 34.6 all-reduce.5
